TPU v7x, 128 devices: a whole 4x4x4 slice. The times are simulated.
128 devices in a mesh: heads: 8 (over z, core), tok: 16 (over y, x).
Axes of the slice: x: 4, y: 4, z: 4, core: 2. Of those that a mesh axis runs over, the one named last changes fastest.
Arguments:
- states: bfloat16 [512, 7168], P('heads', 'tok'), may hold values from -10 to 10
- key_values: bfloat16 [2, 2, 8192, 7168], P(None, None, 'tok', 'heads')
- cache_length: int32 [2], replicated, may hold values from 0 to 7936, as said below
- norm1_gain: float32 [7168], replicated, may hold values from 0.25 to 1.75
- norm1_bias: float32 [7168], replicated, may hold values from -3 to 3
- qkv_weight: bfloat16 [7168, 3, 7168], P('tok', None, 'heads'), may hold values from -0.0625 to 0.0625
- qkv_bias: float32 [3, 7168], P(None, 'heads'), may hold values from -3 to 3
- out_weight: bfloat16 [7168, 7168], P('heads', 'tok'), may hold values from -0.0625 to 0.0625
- out_bias: float32 [7168], P('tok'), may hold values from -3 to 3
- norm2_gain: float32 [7168], replicated, may hold values from 0.25 to 1.75
- norm2_bias: float32 [7168], replicated, may hold values from -3 to 3
- fc1_weight: bfloat16 [7168, 28672], P(None, ('heads', 'tok')), may hold values from -0.0625 to 0.0625
- fc1_bias: float32 [28672], P(('heads', 'tok')), may hold values from -3 to 3
- fc2_weight: bfloat16 [28672, 7168], P(('heads', 'tok')), may hold values from -0.03125 to 0.03125
- fc2_bias: float32 [7168], P('tok'), may hold values from -3 to 3
Outputs:
- hidden_out: bfloat16 [512, 7168], P('heads', 'tok')
- cache_out: bfloat16 [2, 2, 8192, 7168], P(None, None, 'tok', 'heads')
Inputs may be any that keep to these rules, and one draw needn't show every extreme that they name: Request r's new tokens take positions cache_length[r] to cache_length[r] + 255 of its cache; some request reaches the largest length.
All inputs are finite; a program needn't handle non-finite values.
Results may differ from a plain program's by a relative error of at most 0.013.
The roundings to bfloat16 on the way count: a program that leaves them out, or rounds other values in their place, can miss the bound.
Values may be sent and summed in bfloat16 or wider, within the bound.
A program may use at most 192 MiB of HBM per device.

v0:
```python
import jax
import jax.numpy as jnp
from jax import lax
from jax.sharding import PartitionSpec as P

HD = 128
SINK = 4
REQS = 2
NEW = 256
EPSILON = 1e-05
NEGATIVE = -1e30


def joined(value, axis, join):
    pieces = jax.tree.map(lambda part: lax.all_gather(part, axis), value)
    head = jax.tree.map(lambda part: part[0], pieces)
    tail = jax.tree.map(lambda part: part[1:], pieces)
    so_far, _ = lax.scan(lambda so_far, section: (join(so_far, section), None), head, tail)
    return so_far


def norm_rows(values, total_sum, total_square, width, gain, shift):
    mean_row = total_sum / width
    variance = total_square / width - mean_row * mean_row
    return (
        (values - mean_row[:, None]) * lax.rsqrt(variance[:, None] + EPSILON) * gain + shift
    ).astype(jnp.bfloat16)


def merge_parts(first, second):
    highest = jnp.maximum(first[1], second[1])
    left_factor = jnp.exp(first[1] - highest)
    right_factor = jnp.exp(second[1] - highest)
    return (
        first[0] * left_factor[..., None] + second[0] * right_factor[..., None],
        highest,
        first[2] * left_factor + second[2] * right_factor,
    )


def shards(
    states,
    key_values,
    cache_length,
    norm1_gain,
    norm1_bias,
    qkv_weight,
    qkv_bias,
    out_weight,
    out_bias,
    norm2_gain,
    norm2_bias,
    fc1_weight,
    fc1_bias,
    fc2_weight,
    fc2_bias,
):
    head_count = lax.axis_size("heads")
    tok_count = lax.axis_size("tok")
    tok_index = lax.axis_index("tok")
    rows_local, cols_local = states.shape
    width = cols_local * tok_count
    group = qkv_weight.shape[2]
    group_heads = group // HD
    tokens = rows_local * head_count
    cache_rows = key_values.shape[2]
    window = cache_rows * tok_count // 2
    col_start = tok_index * cols_local
    states_float = states.astype(jnp.float32)
    row_sum, row_square = lax.psum(
        (jnp.sum(states_float, axis=1), jnp.sum(states_float * states_float, axis=1)), "tok"
    )
    gain_one = lax.dynamic_slice_in_dim(norm1_gain, col_start, cols_local)
    shift_one = lax.dynamic_slice_in_dim(norm1_bias, col_start, cols_local)
    normed_one = norm_rows(states_float, row_sum, row_square, width, gain_one, shift_one)
    gathered = lax.all_gather(normed_one, "heads", axis=0, tiled=True)
    weight_flat = qkv_weight.reshape(cols_local, 3 * group)
    factors = jnp.asarray([HD ** (-0.5), 1.0, 1.0], dtype=jnp.float32)[None, :, None]
    partial_qkv = jnp.dot(gathered, weight_flat, preferred_element_type=jnp.float32)
    summed = lax.psum(partial_qkv, "tok")
    projected = ((summed.reshape(tokens, 3, group) + qkv_bias[None]) * factors).astype(jnp.bfloat16)
    queries = projected[:, 0].reshape(REQS, NEW, group_heads, HD)
    fresh = jnp.moveaxis(projected[:, 1:].reshape(REQS, NEW, 2, group), 2, 0)
    key_pos = tok_index * cache_rows + jnp.arange(cache_rows, dtype=jnp.int32)
    appended_parts = []
    for request in range(REQS):
        offset = key_pos - cache_length[request]
        inside = (offset >= 0) & (offset < NEW)
        picked = jnp.take(fresh[:, request], jnp.clip(offset, 0, NEW - 1), axis=1)
        appended_parts.append(jnp.where(inside[None, :, None], picked, key_values[:, request]))
    appended = jnp.stack(appended_parts, axis=1)
    keys = appended[0].reshape(REQS, cache_rows, group_heads, HD)
    values = appended[1].reshape(REQS, cache_rows, group_heads, HD)
    query_pos = cache_length[:, None] + jnp.arange(NEW, dtype=jnp.int32)[None, :]
    distance = query_pos[:, :, None] - key_pos[None, None, :]
    allowed = (distance >= 0) & ((key_pos[None, None, :] < SINK) | (distance < window))
    scores = jnp.einsum("rshd,rphd->rshp", queries, keys, preferred_element_type=jnp.float32)
    masked = jnp.where(allowed[:, :, None, :], scores, NEGATIVE)
    peak = jnp.max(masked, axis=-1)
    weights = jnp.where(allowed[:, :, None, :], jnp.exp(masked - peak[..., None]), 0.0)
    totals = jnp.sum(weights, axis=-1)
    partial_out = jnp.einsum(
        "rshp,rphd->rshd", weights.astype(jnp.bfloat16), values, preferred_element_type=jnp.float32
    )
    merged, highest, denominator = joined((partial_out, peak, totals), "tok", merge_parts)
    attended = (merged / denominator[..., None]).astype(jnp.bfloat16).reshape(tokens, group)
    projected_out = lax.psum_scatter(
        jnp.dot(attended, out_weight, preferred_element_type=jnp.float32),
        "heads",
        scatter_dimension=0,
        tiled=True,
    )
    residual = (states_float + projected_out + out_bias).astype(jnp.bfloat16)
    residual_float = residual.astype(jnp.float32)
    second_sum, second_square = lax.psum(
        (jnp.sum(residual_float, axis=1), jnp.sum(residual_float * residual_float, axis=1)), "tok"
    )
    gain_two = lax.dynamic_slice_in_dim(norm2_gain, col_start, cols_local)
    shift_two = lax.dynamic_slice_in_dim(norm2_bias, col_start, cols_local)
    normed_part = norm_rows(residual_float, second_sum, second_square, width, gain_two, shift_two)
    normed = lax.all_gather(normed_part, "tok", axis=1, tiled=True)
    active = jnp.maximum(
        jnp.dot(
            lax.all_gather(normed, "heads", axis=0, tiled=True),
            fc1_weight,
            preferred_element_type=jnp.float32,
        )
        + fc1_bias,
        0.0,
    ).astype(jnp.bfloat16)
    hidden_local = fc1_weight.shape[1]
    term = jnp.einsum(
        "hnf,ftc->htnc",
        active.reshape(head_count, rows_local, hidden_local),
        fc2_weight.reshape(hidden_local, tok_count, cols_local),
        preferred_element_type=jnp.float32,
    )
    down = lax.psum_scatter(
        term.reshape(head_count * tok_count * rows_local, cols_local),
        ("heads", "tok"),
        scatter_dimension=0,
        tiled=True,
    )
    hidden_out = (residual_float + down + fc2_bias).astype(jnp.bfloat16)
    return (hidden_out, appended)


def solution(mesh):
    placed = (
        P("heads", "tok"),
        P(None, None, "tok", "heads"),
        P(),
        P(),
        P(),
        P("tok", None, "heads"),
        P(None, "heads"),
        P("heads", "tok"),
        P("tok"),
        P(),
        P(),
        P(None, ("heads", "tok")),
        P(("heads", "tok")),
        P(("heads", "tok"), None),
        P("tok"),
    )
    return jax.shard_map(
        shards,
        mesh=mesh,
        in_specs=placed,
        out_specs=(P("heads", "tok"), P(None, None, "tok", "heads")),
        check_vma=False,
    )
```

profile of v0, /device:TPU:0, one launch (start us, length us, event | category | flops | bytes accessed | tf_op | source)
XLA Modules:
  0.0 1517.9 jit_solution(4574828928947439626)
XLA Ops:
  9.9 40.7 %all-reduce.1 = (f32[64]{0:T(128)S(1)}, f32[64]{0:T(128)S(1)}) all-reduce(f32[64]{0:T(128)S(1)} %get-tuple-element.71, f32[64]{0:T(128)S(1)} %get-tuple-element.70), channel_id=1, replica_groups=mesh['heads'=8,'tok'=16] {'tok'}, use_global_device_ids=true, to_apply=%region_3.0 | all-reduce | flops 128 | bytes 1024 | tf_op jit(solution)/shard_map/psum | solution.py:70
  51.6 15.4 %all_gather.27 = bf16[512,448]{1,0:T(8,128)(2,1)} all-gather(bf16[64,448]{1,0:T(8,128)(2,1)S(1)} %fusion.33), channel_id=1, replica_groups=mesh['heads'=8,'tok'=16] {'heads'}, dimensions={0}, use_global_device_ids=true | all-gather | bytes 516096 | tf_op jit(solution)/shard_map/all_gather | solution.py:76
  67.0 4.4 copy.45
  71.3 6.0 fusion.60
  83.0 4.3 fusion.58
  87.2 101.3 %all-reduce.4.cloned.1.call-done = f32[512,3,896]{0,2,1:T(8,128)} async-done(((f32[512,3,896]{0,2,1:T(8,128)}), f32[512,3,896]{0,2,1:T(8,128)}) %all-reduce.4.cloned.1.call-update) | async-done | bytes 5505040 | tf_op jit(solution)/shard_map/psum | solution.py:80
  188.6 3.1 multiply_convert_fusion
  194.0 6.1 copy.47
  200.1 4.0 slice_bitcast_fusion.1
  204.1 6.9 gather_fusion
  211.0 6.8 gather_fusion.1
  217.8 17.6 %fusion.16 = (bf16[2,1,512,896]{3,0,2,1:T(2,128)(2,1)S(1)}, bf16[2,1,512,896]{3,0,2,1:T(2,128)(2,1)S(1)}) fusion(bf16[2,1,512,896]{3,2,1,0:T(8,128)(2,1)} %get-tuple-element.99, bf16[512,2,896]{2,1,0:T(2,128)(2,1)} %gather_fusion, pred[512]{0:T(512)(128)(4,1)S(1)} %compare_and_fusion.1, pred[512]{0:T(512)(128)(4,1)S(1)} %fusion.53, ...), kind=kLoop, calls=%fused_computation.38 | loop fusion | flops 3670016 | bytes 11012096 | tf_op jit(solution)/shard_map/stack | solution.py:91
  235.4 11.7 slice_maximum_fusion
  247.1 9.3 copy.50
  256.4 9.3 copy.51
  265.7 3.1 reshape_squeeze.11
  268.8 3.2 fusion.4
  275.0 3.0 fusion.18
  280.8 23.8 %all-gather.1 = f32[32,256,7]{1,2,0:T(8,128)S(1)} all-gather(f32[2,256,7]{1,2,0:T(8,128)S(1)} %get-tuple-element.109), channel_id=3, replica_groups=mesh['heads'=8,'tok'=16] {'tok'}, dimensions={0}, use_global_device_ids=true | all-gather | bytes 243712 | tf_op jit(solution)/shard_map/all_gather | solution.py:15
  305.3 4.7 fusion.5
  310.0 22.1 %all-gather.2 = f32[32,256,7]{1,2,0:T(8,128)S(1)} all-gather(f32[2,256,7]{1,2,0:T(8,128)S(1)} %fusion.5), channel_id=4, replica_groups=mesh['heads'=8,'tok'=16] {'tok'}, dimensions={0}, use_global_device_ids=true | all-gather | bytes 243712 | tf_op jit(solution)/shard_map/all_gather | solution.py:15
  333.9 124.0 %all-gather.9.cloned.1.call-done = f32[32,256,7,128]{3,1,2,0:T(8,128)} async-done(((f32[2,256,7,128]{3,1,2,0:T(8,128)}), f32[32,256,7,128]{3,1,2,0:T(8,128)}) %all-gather.9.cloned.1.call-update) | async-done | bytes 29360144 | tf_op jit(solution)/shard_map/all_gather | solution.py:15
  461.8 20.8 %slice.86 = f32[30,256,7,128]{3,1,2,0:T(8,128)} slice(f32[32,256,7,128]{3,1,2,0:T(8,128)} %all-gather.9.cloned.1.call-done), slice={[2:32], [0:256], [0:7], [0:128]} | slice | bytes 55050240 | tf_op jit(solution)/shard_map/slice | solution.py:17
  482.6 185.3 %while.14 = (s32[]{:T(128)}, f32[2,256,7,128]{3,2,1,0:T(8,128)}, f32[2,256,7]{2,1,0:T(8,128)}, f32[2,256,7]{2,1,0:T(8,128)}, f32[15,2,256,7]{2,3,1,0:T(8,128)}, ...) while((s32[]{:T(128)}, f32[2,256,7,128]{3,2,1,0:T(8,128)}, ...), condition=%wide.region_8.10_spmd, body=%wide.region_7.9_spmd.sunk | while | flops 1397762 | bytes 18493624 | solution.py:18
  482.6 3.0 constant_dynamic-slice_fusion.5
  489.6 5.4 fusion.72
  495.0 3.0 constant_dynamic-slice_fusion.5
  501.9 5.4 fusion.72
  507.3 3.0 constant_dynamic-slice_fusion.5
  514.3 5.4 fusion.72
  519.7 3.0 constant_dynamic-slice_fusion.5
  526.6 5.4 fusion.72
  532.0 3.0 constant_dynamic-slice_fusion.5
  539.0 5.4 fusion.72
  544.4 3.0 constant_dynamic-slice_fusion.5
  551.3 5.4 fusion.72
  556.7 3.0 constant_dynamic-slice_fusion.5
  563.7 5.4 fusion.72
  569.1 3.0 constant_dynamic-slice_fusion.5
  576.0 5.4 fusion.72
  581.5 3.0 constant_dynamic-slice_fusion.5
  588.4 5.4 fusion.72
  593.8 3.0 constant_dynamic-slice_fusion.5
  600.7 5.4 fusion.72
  606.2 3.0 constant_dynamic-slice_fusion.5
  613.1 5.4 fusion.72
  618.5 3.0 constant_dynamic-slice_fusion.5
  625.4 5.4 fusion.72
  630.9 3.0 constant_dynamic-slice_fusion.5
  637.8 5.4 fusion.72
  643.2 3.0 constant_dynamic-slice_fusion.5
  650.1 5.4 fusion.72
  655.6 3.0 constant_dynamic-slice_fusion.5
  662.5 5.4 fusion.72
  673.3 30.4 %reduce-scatter.3.cloned.1.call-done = f32[64,448]{1,0:T(8,128)} async-done(((f32[512,448]{1,0:T(8,128)}), f32[64,448]{1,0:T(8,128)}) %reduce-scatter.3.cloned.1.call-update) | async-done | bytes 114704 | tf_op jit(solution)/shard_map/reduce_scatter | solution.py:107
  704.8 40.2 %all-reduce = (f32[64]{0:T(128)S(1)}, f32[64]{0:T(128)S(1)}) all-reduce(f32[64]{0:T(128)S(1)} %get-tuple-element.69, f32[64]{0:T(128)S(1)} %get-tuple-element.68), channel_id=1, replica_groups=mesh['heads'=8,'tok'=16] {'tok'}, use_global_device_ids=true, to_apply=%region_13.15 | all-reduce | flops 128 | bytes 1024 | tf_op jit(solution)/shard_map/psum | solution.py:115
  745.1 21.6 %all-gather.3 = bf16[16,448,64]{1,2,0:T(8,128)(2,1)S(1)} all-gather(bf16[1,448,64]{1,2,0:T(8,128)(2,1)S(1)} %fusion.44), channel_id=1, replica_groups=mesh['heads'=8,'tok'=16] {'tok'}, dimensions={0}, use_global_device_ids=true | all-gather | bytes 974848 | tf_op jit(solution)/shard_map/all_gather | solution.py:121
  768.3 3.0 reshape.137
  771.3 7.5 reshape.104
  778.8 35.7 %all-gather.7.cloned.1.call-done = bf16[512,7168]{1,0:T(8,128)(2,1)} async-done(((bf16[64,7168]{1,0:T(8,128)(2,1)}), bf16[512,7168]{1,0:T(8,128)(2,1)}) %all-gather.7.cloned.1.call-update) | async-done | bytes 7340048 | tf_op jit(solution)/shard_map/all_gather | solution.py:124
  814.5 6.1 fusion.22
  821.7 13.0 fusion.9
  834.7 7.6 pad_maximum_fusion
  844.6 665.0 %reduce-scatter.5.cloned.1.call-done = f32[64,448]{1,0:T(8,128)} async-done(((f32[8192,448]{1,0:T(8,128)}), f32[64,448]{1,0:T(8,128)}) %reduce-scatter.5.cloned.1.call-update) | async-done | bytes 114704 | tf_op jit(solution)/shard_map/reduce_scatter | solution.py:138
  (227 shorter events, 95.2 us)
Async XLA Ops:
  7.2 807.3 %copy-start = (bf16[7168,224]{0,1:T(8,128)(2,1)S(1)}, bf16[7168,224]{0,1:T(8,128)(2,1)}, u32[]{:S(2)}) copy-start(bf16[7168,224]{0,1:T(8,128)(2,1)} %param.31) | copy-start | bytes 9633796
  7.2 181.4 %all-reduce.4.cloned.1.call-start = ((), (), s32[]{:S(2)}) async-start(), calls=%async_computation.2 | async-start | bytes 11010048 | tf_op jit(solution)/shard_map/psum | solution.py:80
  77.3 0.7 copy-start.10
  77.3 380.6 %all-gather.9.cloned.1.call-start = ((), (), s32[]{:S(2)}) async-start(), calls=%async_computation.6 | async-start | bytes 31195136 | tf_op jit(solution)/shard_map/all_gather | solution.py:15
  82.9 105.6 %copy-start.9 = (f32[3,896]{1,0:T(4,128)S(1)}, f32[3,896]{1,0:T(4,128)}, u32[]{:S(2)}) copy-start(f32[3,896]{1,0:T(4,128)} %param.26) | copy-start | bytes 32260
  83.0 105.6 %copy-start.13 = (f32[3]{0:T(128)S(1)}, f32[3]{0:T(128)}, u32[]{:S(2)}) copy-start(f32[3]{0:T(128)} %constant.59.clone) | copy-start | bytes 40
  235.4 11.7 copy-start.3
  235.4 11.7 copy-start.4
  268.8 6.2 copy-start.5
  272.0 3.0 copy-start.2
  280.8 422.9 %reduce-scatter.3.cloned.1.call-start = ((), (), s32[]{:S(2)}) async-start(), calls=%async_computation.3 | async-start | bytes 1179648 | tf_op jit(solution)/shard_map/reduce_scatter | solution.py:107
  457.9 1.5 slice-start
  482.6 3.7 copy-start.7
  487.4 2.1 copy-start.1
  489.5 5.4 copy-start.8
  495.0 3.7 copy-start.7
  499.8 2.1 copy-start.1
  501.9 5.4 copy-start.8
  507.3 3.7 copy-start.7
  512.1 2.1 copy-start.1
  514.3 5.4 copy-start.8
  519.7 3.7 copy-start.7
  524.5 2.1 copy-start.1
  526.6 5.4 copy-start.8
  532.0 3.7 copy-start.7
  536.8 2.1 copy-start.1
  539.0 5.4 copy-start.8
  544.4 3.7 copy-start.7
  549.2 2.1 copy-start.1
  551.3 5.4 copy-start.8
  556.7 3.7 copy-start.7
  561.5 2.1 copy-start.1
  563.7 5.4 copy-start.8
  569.1 3.7 copy-start.7
  573.9 2.1 copy-start.1
  576.0 5.4 copy-start.8
  581.5 3.7 copy-start.7
  586.2 2.1 copy-start.1
  588.4 5.4 copy-start.8
  593.8 3.7 copy-start.7
  598.6 2.1 copy-start.1
  600.7 5.4 copy-start.8
  606.2 3.7 copy-start.7
  610.9 2.1 copy-start.1
  613.1 5.4 copy-start.8
  618.5 3.7 copy-start.7
  623.3 2.1 copy-start.1
  625.4 5.4 copy-start.8
  630.9 3.7 copy-start.7
  635.6 2.1 copy-start.1
  637.8 5.4 copy-start.8
  643.2 3.7 copy-start.7
  648.0 2.1 copy-start.1
  650.1 5.4 copy-start.8
  655.6 3.7 copy-start.7
  660.3 2.1 copy-start.1
  662.5 5.4 copy-start.8
  667.9 2.1 copy-start.14
  670.0 33.8 %copy-start.6 = (bf16[64,448]{1,0:T(8,128)(2,1)S(1)}, bf16[64,448]{1,0:T(8,128)(2,1)}, u32[]{:S(2)}) copy-start(bf16[64,448]{1,0:T(8,128)(2,1)} %param.20) | copy-start | bytes 172036
  670.0 33.8 %copy-start.11 = (f32[448]{0:T(512)S(1)}, f32[448]{0:T(512)}, u32[]{:S(2)}) copy-start(f32[448]{0:T(512)} %param.28) | copy-start | bytes 5380
  671.7 142.8 %all-gather.7.cloned.1.call-start = ((), (), s32[]{:S(2)}) async-start(), calls=%async_computation.4 | async-start | bytes 8257536 | tf_op jit(solution)/shard_map/all_gather | solution.py:124
  771.2 43.2 %copy-start.15 = (f32[224]{0:T(256)S(1)}, f32[224]{0:T(256)}, u32[]{:S(2)}) copy-start(f32[224]{0:T(256)} %param.32) | copy-start | bytes 2692
  771.3 738.4 %reduce-scatter.5.cloned.1.call-start = ((), (), s32[]{:S(2)}) async-start(), calls=%async_computation.5 | async-start | bytes 16908288 | tf_op jit(solution)/shard_map/reduce_scatter | solution.py:138
  842.3 667.3 %copy-start.12 = (f32[448]{0:T(512)S(1)}, f32[448]{0:T(512)}, u32[]{:S(2)}) copy-start(f32[448]{0:T(512)} %param.34) | copy-start | bytes 5380
Sparse Core Ops, SparseCore 0:
  77.5 111.0 all-reduce.3
  280.9 176.9 all-gather.8
  671.8 31.8 reduce-scatter.2
  771.4 43.0 all-gather.6
  834.8 674.7 reduce-scatter.4
where the time goes:
time: 1530 us; the launch traced here: 1520 us
  waiting for transfers between devices  957 us (63%)
  local copies, waits for them, and re-layouts  181 us (12%)
  other arithmetic  169 us (11%)
  blocking collectives  164 us (11%)
  matrix products  33 us (2%)
    reduce_scatter x1, waiting for transfers between devices, shards(): lax.psum_scatter(term.reshape(head_count * tok_count * rows_local, cols_l...  665 us
    all_gather x1, waiting for transfers between devices, joined(): pieces = jax.tree.map(lambda part: lax.all_gather(part, axis), value)  124 us
    psum x1, waiting for transfers between devices, shards(): summed = lax.psum(partial_qkv, 'tok')  101 us
    add x15, other arithmetic, merge_parts(): first[0] * left_factor[..., None] + second[0] * right_factor[..., None]  81.5 us
    dynamic_slice x60, local copies, waits for them, and re-layouts, joined(): lax.scan(lambda so_far, section: (join(so_far, section), None), head, tail)  71.5 us
    all_gather x2, blocking collectives, joined(): pieces = jax.tree.map(lambda part: lax.all_gather(part, axis), value)  45.8 us
    psum x1, blocking collectives, shards(): lax.psum((jnp.sum(states_float, axis=1), jnp.sum(states_float * states_fl...  40.7 us
    psum x1, blocking collectives, shards(): lax.psum((jnp.sum(residual_float, axis=1), jnp.sum(residual_float * resid...  40.2 us
  transfers between devices with their start and end apart: 5, of which 5 were waited for; matrix products, arithmetic and copies ran while one was open for 2% of the time, Pallas kernels for 0%

commit v1 on v0

--- a/solution.py
+++ b/solution.py
@@ -77,7 +77,7 @@
     weight_flat = qkv_weight.reshape(cols_local, 3 * group)
     factors = jnp.asarray([HD ** (-0.5), 1.0, 1.0], dtype=jnp.float32)[None, :, None]
     partial_qkv = jnp.dot(gathered, weight_flat, preferred_element_type=jnp.float32)
-    summed = lax.psum(partial_qkv, "tok")
+    summed = jnp.sum(lax.all_gather(partial_qkv, "tok"), axis=0)
     projected = ((summed.reshape(tokens, 3, group) + qkv_bias[None]) * factors).astype(jnp.bfloat16)
     queries = projected[:, 0].reshape(REQS, NEW, group_heads, HD)
     fresh = jnp.moveaxis(projected[:, 1:].reshape(REQS, NEW, 2, group), 2, 0)

time: 1530 us -> 1860 us (1.22)
  waiting for transfers between devices: 957 us -> 1320 us
  other arithmetic: 169 us -> 142 us
    all_gather x0 -> x1, waiting for transfers between devices: none -> 460 us  [shards(): summed = jnp.sum(lax.all_gather(partial_qkv, 'tok'), axis=0)]
    psum x1 -> x0, waiting for transfers between devices: 101 us -> none  [shards(): summed = lax.psum(partial_qkv, 'tok')]
    add x15, other arithmetic: 81.5 us -> 24.5 us  [merge_parts(): first[0] * left_factor[..., None] + second[0] * right_factor[..., None]]
    reduce_sum x0 -> x1, other arithmetic: none -> 30.1 us  [shards(): summed = jnp.sum(lax.all_gather(partial_qkv, 'tok'), axis=0)]
    dynamic_slice x60, local copies, waits for them, and re-layouts: 71.5 us -> 50.2 us  [joined(): lax.scan(lambda so_far, section: (join(so_far, section), None), head, tail)]
    while x90 -> x120, local copies, waits for them, and re-layouts: 0.17 us -> 19.9 us
where the time goes in v1:
time: 1860 us
  waiting for transfers between devices  1320 us (71%)
  local copies, waits for them, and re-layouts  186 us (10%)
  blocking collectives  164 us (9%)
  other arithmetic  142 us (8%)
  matrix products  33.1 us (2%)
    reduce_scatter x1, waiting for transfers between devices, shards(): lax.psum_scatter(term.reshape(head_count * tok_count * rows_local, cols_l...  665 us
    all_gather x1, waiting for transfers between devices, shards(): summed = jnp.sum(lax.all_gather(partial_qkv, 'tok'), axis=0)  460 us
    all_gather x1, waiting for transfers between devices, joined(): pieces = jax.tree.map(lambda part: lax.all_gather(part, axis), value)  124 us
    dynamic_slice x60, local copies, waits for them, and re-layouts, joined(): lax.scan(lambda so_far, section: (join(so_far, section), None), head, tail)  50.2 us
    all_gather x2, blocking collectives, joined(): pieces = jax.tree.map(lambda part: lax.all_gather(part, axis), value)  46.1 us
    psum x1, blocking collectives, shards(): lax.psum((jnp.sum(states_float, axis=1), jnp.sum(states_float * states_fl...  40.7 us
    psum x1, blocking collectives, shards(): lax.psum((jnp.sum(residual_float, axis=1), jnp.sum(residual_float * resid...  40.2 us
  transfers between devices with their start and end apart: 5, of which 5 were waited for; matrix products, arithmetic and copies ran while one was open for 2% of the time, Pallas kernels for 0%

profile of v1, /device:TPU:0, one launch (start us, length us, event | category | flops | bytes accessed | tf_op | source)
XLA Modules:
  0.0 1856.8 jit_solution(4599868131708025216)
XLA Ops:
  9.9 40.7 %all-reduce.1 = (f32[64]{0:T(128)S(1)}, f32[64]{0:T(128)S(1)}) all-reduce(f32[64]{0:T(128)S(1)} %get-tuple-element.71, f32[64]{0:T(128)S(1)} %get-tuple-element.70), channel_id=1, replica_groups=mesh['heads'=8,'tok'=16] {'tok'}, use_global_device_ids=true, to_apply=%region_3.0 | all-reduce | flops 128 | bytes 1024 | tf_op jit(solution)/shard_map/psum | solution.py:70
  51.6 15.4 all_gather.33
  67.0 4.4 copy.44
  71.3 6.0 fusion.60
  83.1 5.6 fusion.58
  88.7 460.2 %all-gather.11.cloned.1.call-done = f32[8192,2688]{1,0:T(8,128)} async-done(((f32[512,2688]{1,0:T(8,128)}), f32[8192,2688]{1,0:T(8,128)}) %all-gather.11.cloned.1.call-update) | async-done | bytes 88080400 | tf_op jit(solution)/shard_map/all_gather | solution.py:80
  548.9 30.1 %reduce_sum.56 = f32[512,2688]{1,0:T(8,128)} reduce(f32[16,512,2688]{2,1,0:T(8,128)} %bitcast.5, f32[]{:T(128)} %constant.14.clone.1), dimensions={0}, to_apply=%region_4.0 | reduce | flops 20643840 | bytes 93585408 | tf_op jit(solution)/shard_map/reduce_sum | solution.py:80
  579.0 6.2 copy.45
  585.2 3.1 multiply_convert_fusion
  590.6 5.6 copy.46
  596.2 4.0 slice_bitcast_fusion.1
  600.2 6.8 gather_fusion
  607.1 6.8 gather_fusion.1
  613.9 17.7 fusion.16
  631.7 11.5 slice_maximum_fusion
  643.2 9.3 copy.50
  652.5 3.2 reshape_squeeze.11
  655.7 9.3 copy.49
  665.0 3.2 fusion.4
  668.2 2.9 copy-done.3
  671.1 3.0 fusion.18
  674.2 2.8 copy.54
  677.0 4.6 fusion.5
  681.6 23.9 %all-gather.3 = f32[32,256,7]{1,2,0:T(8,128)S(1)} all-gather(f32[2,256,7]{1,2,0:T(8,128)S(1)} %fusion.5), channel_id=5, replica_groups=mesh['heads'=8,'tok'=16] {'tok'}, dimensions={0}, use_global_device_ids=true | all-gather | bytes 243712 | tf_op jit(solution)/shard_map/all_gather | solution.py:15
  705.5 22.2 %all-gather.2 = f32[32,256,7]{1,2,0:T(8,128)S(1)} all-gather(f32[2,256,7]{1,2,0:T(8,128)S(1)} %get-tuple-element.109), channel_id=4, replica_groups=mesh['heads'=8,'tok'=16] {'tok'}, dimensions={0}, use_global_device_ids=true | all-gather | bytes 243712 | tf_op jit(solution)/shard_map/all_gather | solution.py:15
  730.2 124.4 %all-gather.13.cloned.1.call-done = f32[32,256,7,128]{3,1,2,0:T(8,128)} async-done(((f32[2,256,7,128]{3,1,2,0:T(8,128)}), f32[32,256,7,128]{3,1,2,0:T(8,128)}) %all-gather.13.cloned.1.call-update) | async-done | bytes 29360144 | tf_op jit(solution)/shard_map/all_gather | solution.py:15
  856.1 2.4 copy.55
  858.5 20.9 %slice.86 = f32[30,256,7,128]{3,1,2,0:T(8,128)} slice(f32[32,256,7,128]{3,1,2,0:T(8,128)} %all-gather.13.cloned.1.call-done), slice={[2:32], [0:256], [0:7], [0:128]} | slice | bytes 55050240 | tf_op jit(solution)/shard_map/slice | solution.py:17
  879.3 127.5 %while.14 = (s32[]{:T(128)}, f32[2,256,7,128]{3,2,1,0:T(8,128)}, f32[2,256,7]{2,1,0:T(8,128)}, f32[2,256,7]{2,1,0:T(8,128)}, f32[15,2,256,7]{2,3,1,0:T(8,128)}, ...) while((s32[]{:T(128)}, f32[2,256,7,128]{3,2,1,0:T(8,128)}, ...), condition=%wide.region_8.10_spmd, body=%wide.region_7.9_spmd.sunk | while | flops 1397762 | bytes 25833676 | solution.py:18
  881.1 2.1 fusion.71
  884.9 1.6 fusion.72
  889.6 2.1 fusion.71
  893.4 1.6 fusion.72
  898.1 2.1 fusion.71
  901.9 1.6 fusion.72
  906.6 2.1 fusion.71
  910.4 1.6 fusion.72
  915.1 2.1 fusion.71
  918.9 1.6 fusion.72
  923.6 2.1 fusion.71
  927.4 1.6 fusion.72
  932.1 2.1 fusion.71
  935.9 1.6 fusion.72
  940.6 2.1 fusion.71
  949.1 2.1 fusion.71
  957.6 2.1 fusion.71
  966.1 2.1 fusion.71
  974.6 2.1 fusion.71
  983.1 2.1 fusion.71
  991.6 2.1 fusion.71
  1000.1 2.1 fusion.71
  1006.9 2.0 divide_convert_fusion
  1009.0 1.7 fusion.25
  1012.3 30.4 %reduce-scatter.3.cloned.1.call-done = f32[64,448]{1,0:T(8,128)} async-done(((f32[512,448]{1,0:T(8,128)}), f32[64,448]{1,0:T(8,128)}) %reduce-scatter.3.cloned.1.call-update) | async-done | bytes 114704 | tf_op jit(solution)/shard_map/reduce_scatter | solution.py:107
  1043.7 40.2 %all-reduce = (f32[64]{0:T(128)S(1)}, f32[64]{0:T(128)S(1)}) all-reduce(f32[64]{0:T(128)S(1)} %get-tuple-element.69, f32[64]{0:T(128)S(1)} %get-tuple-element.68), channel_id=1, replica_groups=mesh['heads'=8,'tok'=16] {'tok'}, use_global_device_ids=true, to_apply=%region_13.15 | all-reduce | flops 128 | bytes 1024 | tf_op jit(solution)/shard_map/psum | solution.py:115
  1084.1 21.6 %all-gather.4 = bf16[16,448,64]{1,2,0:T(8,128)(2,1)S(1)} all-gather(bf16[1,448,64]{1,2,0:T(8,128)(2,1)S(1)} %fusion.44), channel_id=1, replica_groups=mesh['heads'=8,'tok'=16] {'tok'}, dimensions={0}, use_global_device_ids=true | all-gather | bytes 974848 | tf_op jit(solution)/shard_map/all_gather | solution.py:121
  1107.2 3.0 reshape.138
  1110.3 7.5 reshape.104
  1117.7 35.7 %all-gather.9.cloned.1.call-done = bf16[512,7168]{1,0:T(8,128)(2,1)} async-done(((bf16[64,7168]{1,0:T(8,128)(2,1)}), bf16[512,7168]{1,0:T(8,128)(2,1)}) %all-gather.9.cloned.1.call-update) | async-done | bytes 7340048 | tf_op jit(solution)/shard_map/all_gather | solution.py:124
  1153.5 6.1 fusion.22
  1160.7 13.0 fusion.9
  1173.7 7.6 pad_maximum_fusion
  1181.3 2.3 copy.65
  1183.6 664.9 %reduce-scatter.5.cloned.1.call-done = f32[64,448]{1,0:T(8,128)} async-done(((f32[8192,448]{1,0:T(8,128)}), f32[64,448]{1,0:T(8,128)}) %reduce-scatter.5.cloned.1.call-update) | async-done | bytes 114704 | tf_op jit(solution)/shard_map/reduce_scatter | solution.py:138
  (259 shorter events, 105.8 us)
Async XLA Ops:
  7.2 1146.3 %copy-start = (bf16[7168,224]{0,1:T(8,128)(2,1)S(1)}, bf16[7168,224]{0,1:T(8,128)(2,1)}, u32[]{:S(2)}) copy-start(bf16[7168,224]{0,1:T(8,128)(2,1)} %param.31) | copy-start | bytes 9633796
  7.2 541.7 %all-gather.11.cloned.1.call-start = ((), (), s32[]{:S(2)}) async-start(), calls=%async_computation.5 | async-start | bytes 93585408 | tf_op jit(solution)/shard_map/all_gather | solution.py:80
  77.4 777.2 %all-gather.13.cloned.1.call-start = ((), (), s32[]{:S(2)}) async-start(), calls=%async_computation.6 | async-start | bytes 31195136 | tf_op jit(solution)/shard_map/all_gather | solution.py:15
  579.0 6.2 copy-start.10
  579.0 6.2 copy-start.14
  631.6 11.5 copy-start.4
  631.7 11.5 copy-start.5
  665.0 6.2 copy-start.6
  668.2 3.0 copy-start.3
  676.9 365.8 %reduce-scatter.3.cloned.1.call-start = ((), (), s32[]{:S(2)}) async-start(), calls=%async_computation.2 | async-start | bytes 1179648 | tf_op jit(solution)/shard_map/reduce_scatter | solution.py:107
  854.6 1.5 slice-start
  881.1 3.8 copy-start.1
  884.9 3.0 copy-start.9
  886.5 1.3 copy-start.2
  889.6 3.8 copy-start.1
  893.4 3.0 copy-start.9
  895.0 1.3 copy-start.2
  898.1 3.8 copy-start.1
  901.9 3.0 copy-start.9
  903.5 1.3 copy-start.2
  904.9 0.7 copy-start.8
  906.6 3.8 copy-start.1
  910.4 3.0 copy-start.9
  912.0 1.3 copy-start.2
  915.1 3.8 copy-start.1
  918.9 3.0 copy-start.9
  920.5 1.3 copy-start.2
  923.6 3.8 copy-start.1
  927.4 3.0 copy-start.9
  929.0 1.3 copy-start.2
  932.1 3.8 copy-start.1
  935.9 3.0 copy-start.9
  937.5 1.3 copy-start.2
  940.6 3.8 copy-start.1
  944.4 3.0 copy-start.9
  946.0 1.3 copy-start.2
  949.1 3.8 copy-start.1
  952.9 3.0 copy-start.9
  954.5 1.3 copy-start.2
  957.6 3.8 copy-start.1
  961.4 3.0 copy-start.9
  963.0 1.3 copy-start.2
  966.1 3.8 copy-start.1
  969.9 3.0 copy-start.9
  971.5 1.3 copy-start.2
  974.6 3.8 copy-start.1
  978.4 3.0 copy-start.9
  980.0 1.3 copy-start.2
  983.1 3.8 copy-start.1
  986.9 3.0 copy-start.9
  988.6 1.3 copy-start.2
  991.6 3.8 copy-start.1
  995.4 3.0 copy-start.9
  997.1 1.3 copy-start.2
  1000.1 3.8 copy-start.1
  1003.9 3.0 copy-start.9
  1005.6 1.3 copy-start.2
  1006.9 2.1 copy-start.15
  1008.9 33.8 %copy-start.7 = (bf16[64,448]{1,0:T(8,128)(2,1)S(1)}, bf16[64,448]{1,0:T(8,128)(2,1)}, u32[]{:S(2)}) copy-start(bf16[64,448]{1,0:T(8,128)(2,1)} %param.20) | copy-start | bytes 172036
  1008.9 33.8 %copy-start.12 = (f32[448]{0:T(512)S(1)}, f32[448]{0:T(512)}, u32[]{:S(2)}) copy-start(f32[448]{0:T(512)} %param.28) | copy-start | bytes 5380
  1010.7 142.8 %all-gather.9.cloned.1.call-start = ((), (), s32[]{:S(2)}) async-start(), calls=%async_computation.3 | async-start | bytes 8257536 | tf_op jit(solution)/shard_map/all_gather | solution.py:124
  1110.2 43.2 %copy-start.16 = (f32[224]{0:T(256)S(1)}, f32[224]{0:T(256)}, u32[]{:S(2)}) copy-start(f32[224]{0:T(256)} %param.32) | copy-start | bytes 2692
  1110.2 738.2 %reduce-scatter.5.cloned.1.call-start = ((), (), s32[]{:S(2)}) async-start(), calls=%async_computation.4 | async-start | bytes 16908288 | tf_op jit(solution)/shard_map/reduce_scatter | solution.py:138
  1181.3 667.2 %copy-start.13 = (f32[448]{0:T(512)S(1)}, f32[448]{0:T(512)}, u32[]{:S(2)}) copy-start(f32[448]{0:T(512)} %param.34) | copy-start | bytes 5380
  (15 other events, 10.8 us)
Sparse Core Ops, SparseCore 0:
  77.5 471.2 all-gather.10
  677.1 177.4 all-gather.12
  1010.8 31.8 reduce-scatter.2
  1110.3 43.0 all-gather.8
  1173.8 674.5 reduce-scatter.4
